TPU v7x, 32 devices: a whole 2x2x4 slice. The times are simulated.
32 devices in a mesh: pages: 2 (over y), rows: 4 (over x, core), cols: 4 (over z).
Axes of the slice: x: 2, y: 2, z: 4, core: 2. Of those that a mesh axis runs over, the one named last changes fastest.
Arguments:
- features: bfloat16 [128, 64, 768], P(('pages', 'rows'), 'cols'), parts along dimension 0, may hold values from -6 to 6
- dw_kernel: bfloat16 [31, 31, 768], P(None, None, ('rows', 'cols')), may hold values from -0.1875 to 0.1875
- w_up: bfloat16 [768, 1536], P(None, ('rows', 'cols')), may hold values from -0.21875 to 0.21875
- w_down: bfloat16 [768, 1536], P(None, ('rows', 'cols')), may hold values from -0.15625 to 0.15625
Outputs:
- block_out: bfloat16 [128, 64, 768], P(('pages', 'rows'), 'cols'), parts along dimension 0
There are 2 independent parts, one for each index of `pages`. A program takes and returns all parts, laid end to end along the dimension named above; an argument that names none is the same for every part. Nothing has to cross between parts.
All inputs are finite; a program needn't handle non-finite values.
Results may differ from a plain program's by a relative error of at most 0.0053.
Values may be sent and summed in bfloat16 or wider, within the bound.
No kernel may reach another device: no remote copies, remote signals or barrier semaphores. Data moves between devices by JAX's collectives and lax.ppermute only.
A program may use at most 64 MiB of HBM per device.

v0:
```python
import jax
import jax.numpy as jnp
from jax import lax
from jax.sharding import PartitionSpec as P


def extended(block, sides, width):
    for axis, dim in sides:
        count = lax.axis_size(axis)
        forward = [(i, i + 1) for i in range(count - 1)]
        backward = [(target, source) for source, target in forward]
        low = lax.ppermute(
            lax.slice_in_dim(block, block.shape[dim] - width, None, axis=dim), axis, forward
        )
        high = lax.ppermute(lax.slice_in_dim(block, 0, width, axis=dim), axis, backward)
        block = jnp.concatenate([low, block, high], axis=dim)
    return block


def expand(normed_rows, piece):
    return jax.nn.gelu(
        jnp.dot(normed_rows, piece, preferred_element_type=jnp.float32), approximate=False
    ).astype(jnp.bfloat16)


def reduce_back(hidden, piece):
    return lax.dot_general(
        hidden, piece, (((1,), (1,)), ((), ())), preferred_element_type=jnp.float32
    )


def on_device(features, dw_kernel, w_up, w_down):
    tile_rows, tile_cols, channels = features.shape
    taps = lax.all_gather(dw_kernel, ("rows", "cols"), axis=2, tiled=True)
    side = taps.shape[0]
    half = (side - 1) // 2
    padded = extended(features, (("rows", 0), ("cols", 1)), half)
    kernel = taps.reshape(side, side, 1, channels)
    mixed = lax.conv_general_dilated(
        padded[None],
        kernel,
        (1, 1),
        "VALID",
        dimension_numbers=("NHWC", "HWIO", "NHWC"),
        feature_group_count=channels,
        preferred_element_type=jnp.float32,
    )[0]
    spread = (features.astype(jnp.float32) + mixed).astype(jnp.bfloat16)
    values = spread.reshape(tile_rows * tile_cols, channels).astype(jnp.float32)
    center = jnp.mean(values, axis=1, keepdims=True)
    spread_sq = jnp.mean((values - center) ** 2, axis=1, keepdims=True)
    normed = ((values - center) * lax.rsqrt(spread_sq + 1e-06)).astype(jnp.bfloat16)
    hidden = expand(normed, lax.all_gather(w_up, ("rows", "cols"), axis=1, tiled=True))
    ffn = reduce_back(hidden, lax.all_gather(w_down, ("rows", "cols"), axis=1, tiled=True))
    result = (values + ffn).astype(jnp.bfloat16)
    return result.reshape(tile_rows, tile_cols, channels)


def solution(mesh):
    return jax.shard_map(
        on_device,
        mesh=mesh,
        in_specs=(
            P(("pages", "rows"), "cols", None),
            P(None, None, ("rows", "cols")),
            P(None, ("rows", "cols")),
            P(None, ("rows", "cols")),
        ),
        out_specs=P(("pages", "rows"), "cols", None),
        check_vma=False,
    )
```

profile of v0, /device:TPU:0, one launch (start us, length us, event | category | flops | bytes accessed | tf_op | source)
XLA Modules:
  0.0 190.2 jit_solution(11549319365002684334)
XLA Ops:
  6.5 0.0 copy-start
  6.5 0.0 all-gather.4.cloned.1.call-start
  6.5 2.4 %copy.11 = bf16[31,31,48]{1,0,2:T(8,128)(2,1)} copy(bf16[31,31,48]{2,1,0:T(8,128)(2,1)} %param.5) | data formatting | bytes 184512 | tf_op args[1]
  9.0 0.0 all-gather.4.cloned.1.call-update
  9.0 0.0 all-gather.8.cloned.1.call-start
  9.0 0.7 all-gather.8.cloned.1.call-update
  9.7 0.0 all-gather.6.cloned.1.call-start
  9.8 0.0 copy-done
  9.8 0.1 fusion.78
  9.9 2.4 %collective-permute-start = (bf16[15,16,768]{2,1,0:T(8,128)(2,1)S(1)}, bf16[15,16,768]{2,1,0:T(8,128)(2,1)S(1)}, u32[]{:S(2)}, u32[]{:S(2)}) collective-permute-start(bf16[15,16,768]{2,1,0:T(8,128)(2,1)S(1)} %get-tuple-element.10), channel_id=1, source_target_pairs={{0,4},{4,8},{8,12},{1,5},{5,9},{9,13},{2,6},{6,10},{10,14},{3,7},{... | collective-permute-start | bytes 1105928 | tf_op jit(solution)/shard_map/ppermute | solution.py:12
  12.3 1.3 collective-permute-start.1
  13.6 0.0 collective-permute-done
  13.7 4.3 %collective-permute-done.1 = bf16[15,16,768]{2,1,0:T(8,128)(2,1)S(1)} collective-permute-done((bf16[15,16,768]{2,1,0:T(8,128)(2,1)S(1)}, bf16[15,16,768]{2,1,0:T(8,128)(2,1)S(1)}, u32[]{:S(2)}, u32[]{:S(2)}) %collective-permute-start.1) | collective-permute-done | bytes 368672 | tf_op jit(solution)/shard_map/ppermute | solution.py:15
  18.0 0.5 fusion.77
  18.4 0.3 copy.8
  18.8 1.3 collective-permute-start.3
  20.1 1.4 copy.7
  21.5 5.5 %collective-permute-start.2 = (bf16[46,15,768]{2,0,1:T(8,128)(2,1)}, bf16[46,15,768]{2,0,1:T(8,128)(2,1)}, u32[]{:S(2)}, u32[]{:S(2)}) collective-permute-start(bf16[46,15,768]{2,0,1:T(8,128)(2,1)} %copy.7), channel_id=1, source_target_pairs={{0,1},{1,2},{2,3},{4,5},{5,6},{6,7},{8,9},{9,10},{10,11},{12,13},{... | collective-permute-start | bytes 3179528 | tf_op jit(solution)/shard_map/ppermute | solution.py:12
  27.0 0.0 all-gather.6.cloned.1.call-update
  27.0 39.9 %collective-permute-done.3 = bf16[46,15,768]{2,0,1:T(8,128)(2,1)} collective-permute-done((bf16[46,15,768]{2,0,1:T(8,128)(2,1)S(1)}, bf16[46,15,768]{2,0,1:T(8,128)(2,1)}, u32[]{:S(2)}, u32[]{:S(2)}) %collective-permute-start.3) | collective-permute-done | bytes 1059872 | tf_op jit(solution)/shard_map/ppermute | solution.py:15
  67.0 1.6 copy.10
  68.5 0.0 collective-permute-done.2
  68.6 1.6 copy.9
  70.1 2.6 %maximum_bitcast_fusion = bf16[1,46,46,768]{3,2,1,0:T(8,128)(2,1)} fusion(bf16[46,15,768]{2,1,0:T(8,128)(2,1)S(1)} %copy.10, bf16[46,16,768]{2,1,0:T(8,128)(2,1)S(1)} %constant_dynamic-update-slice_fusion, bf16[46,15,768]{2,1,0:T(8,128)(2,1)S(1)} %copy.9), kind=kLoop, calls=%fused_computation.2 | loop fusion | flops 9750528 | bytes 6500352 | tf_op jit(solution)/shard_map/broadcast_in_dim | solution.py:40
  72.8 14.1 %all-gather.4.cloned.1.call-done = bf16[31,31,768]{1,0,2:T(8,128)(2,1)} async-done(((bf16[31,31,48]{1,0,2:T(8,128)(2,1)}), bf16[31,31,768]{1,0,2:T(8,128)(2,1)}) %all-gather.4.cloned.1.call-update) | async-done | bytes 1476112 | tf_op jit(solution)/shard_map/all_gather | solution.py:34
  86.8 0.0 copy-start.2
  86.8 12.8 %copy.14 = bf16[31,31,1,768]{3,2,1,0:T(2,128)(2,1)} copy(bf16[31,31,1,768]{1,0,3,2:T(8,128)(2,1)} %bitcast.20) | data formatting | bytes 2952192 | tf_op jit(solution)/shard_map/reshape | solution.py:38
  99.6 0.0 copy-done.2
  99.6 0.0 copy-start.1
  99.6 75.5 %fusion = f32[1,16,16,768]{3,0,2,1:T(1,128)S(1)} fusion(bf16[31,31,1,768]{3,2,1,0:T(2,128)(2,1)} %copy.14, bf16[1,46,46,768]{3,2,1,0:T(8,128)(2,1)S(1)} %copy-done.2), kind=kOutput, calls=%fused_computation | convolution fusion | flops 377880576 | bytes 5512704 | tf_op jit(solution)/shard_map/conv_general_dilated | solution.py:39
  175.1 0.0 copy-done.1
  175.1 0.2 convert_reduce_fusion
  175.3 0.1 div.9
  175.4 0.2 multiply_reduce_fusion
  175.6 0.1 rsqrt.12
  175.7 0.2 fusion.15
  175.9 0.0 all-gather.8.cloned.1.call-done
  176.0 0.0 all-gather.6.cloned.1.call-done
  176.0 7.7 %fusion.12 = bf16[256,768]{1,0:T(8,128)(2,1)} fusion(bf16[768,1536]{0,1:T(8,128)(2,1)} %all-gather.8.cloned.1.call-done, bf16[256,768]{1,0:T(8,128)(2,1)S(1)} %fusion.15, bf16[768,1536]{0,1:T(8,128)(2,1)} %all-gather.6.cloned.1.call-done, bf16[256,768]{1,0:T(8,128)(2,1)S(1)} %bitcast.21), kind=kOutput, calls=%fused_computation.23 | convolution fusion | flops 1234108416 | bytes 5898240 | tf_op jit(solution)/shard_map/dot_general | solution.py:27
  (5 shorter events, 0.1 us)
Async XLA Ops:
  6.5 3.3 %copy-start = (bf16[16,16,768]{2,1,0:T(8,128)(2,1)S(1)}, bf16[16,16,768]{2,1,0:T(8,128)(2,1)}, u32[]{:S(2)}) copy-start(bf16[16,16,768]{2,1,0:T(8,128)(2,1)} %param.4) | copy-start | bytes 1179652
  6.5 80.3 %all-gather.4.cloned.1.call-start = ((), (), s32[]{:S(2)}) async-start(), calls=%async_computation | async-start | bytes 6684672 | tf_op jit(solution)/shard_map/all_gather | solution.py:34
  9.0 167.0 %all-gather.8.cloned.1.call-start = ((), (), s32[]{:S(2)}) async-start(), calls=%async_computation.2 | async-start | bytes 2506752 | tf_op jit(solution)/shard_map/all_gather | solution.py:54
  9.7 166.2 %all-gather.6.cloned.1.call-start = ((), (), s32[]{:S(2)}) async-start(), calls=%async_computation.1 | async-start | bytes 2506752 | tf_op jit(solution)/shard_map/all_gather | solution.py:53
  9.9 3.7 %collective-permute-start = (bf16[15,16,768]{2,1,0:T(8,128)(2,1)S(1)}, bf16[15,16,768]{2,1,0:T(8,128)(2,1)S(1)}, u32[]{:S(2)}, u32[]{:S(2)}) collective-permute-start(bf16[15,16,768]{2,1,0:T(8,128)(2,1)S(1)} %get-tuple-element.10), channel_id=1, source_target_pairs={{0,4},{4,8},{8,12},{1,5},{5,9},{9,13},{2,6},{6,10},{10,14},{3,7},{... | collective-permute-start | bytes 1105928 | tf_op jit(solution)/shard_map/ppermute | solution.py:12
  12.3 5.7 %collective-permute-start.1 = (bf16[15,16,768]{2,1,0:T(8,128)(2,1)S(1)}, bf16[15,16,768]{2,1,0:T(8,128)(2,1)S(1)}, u32[]{:S(2)}, u32[]{:S(2)}) collective-permute-start(bf16[15,16,768]{2,1,0:T(8,128)(2,1)S(1)} %get-tuple-element.9), channel_id=1, source_target_pairs={{4,0},{8,4},{12,8},{5,1},{9,5},{13,9},{6,2},{10,6},{14,10},{7,3},{... | collective-permute-start | bytes 1105928 | tf_op jit(solution)/shard_map/ppermute | solution.py:15
  18.8 48.2 %collective-permute-start.3 = (bf16[46,15,768]{2,0,1:T(8,128)(2,1)S(1)}, bf16[46,15,768]{2,0,1:T(8,128)(2,1)}, u32[]{:S(2)}, u32[]{:S(2)}) collective-permute-start(bf16[46,15,768]{2,0,1:T(8,128)(2,1)S(1)} %copy.8), channel_id=1, source_target_pairs={{1,0},{2,1},{3,2},{5,4},{6,5},{7,6},{9,8},{10,9},{11,10},{13,12},{... | collective-permute-start | bytes 3179528 | tf_op jit(solution)/shard_map/ppermute | solution.py:15
  21.5 47.1 %collective-permute-start.2 = (bf16[46,15,768]{2,0,1:T(8,128)(2,1)}, bf16[46,15,768]{2,0,1:T(8,128)(2,1)}, u32[]{:S(2)}, u32[]{:S(2)}) collective-permute-start(bf16[46,15,768]{2,0,1:T(8,128)(2,1)} %copy.7), channel_id=1, source_target_pairs={{0,1},{1,2},{2,3},{4,5},{5,6},{6,7},{8,9},{9,10},{10,11},{12,13},{... | collective-permute-start | bytes 3179528 | tf_op jit(solution)/shard_map/ppermute | solution.py:12
  86.8 12.8 %copy-start.2 = (bf16[1,46,46,768]{3,2,1,0:T(8,128)(2,1)S(1)}, bf16[1,46,46,768]{3,2,1,0:T(8,128)(2,1)}, u32[]{:S(2)}) copy-start(bf16[1,46,46,768]{3,2,1,0:T(8,128)(2,1)} %maximum_bitcast_fusion) | copy-start | bytes 9750532
  99.6 75.5 %copy-start.1 = (bf16[16,16,768]{2,1,0:T(8,128)(2,1)S(1)}, bf16[16,16,768]{2,1,0:T(8,128)(2,1)}, u32[]{:S(2)}) copy-start(bf16[16,16,768]{2,1,0:T(8,128)(2,1)} %param.4) | copy-start | bytes 1179652
Sparse Core Ops, SparseCore 0:
  9.6 77.1 all-gather.3
  89.1 42.1 all-gather.7
  133.7 41.0 all-gather.5
where the time goes:
time: 191 us; the launch traced here: 190 us
  matrix products  83.2 us (44%)
  waiting for transfers between devices  59 us (31%)
  local copies, waits for them, and re-layouts  20.9 us (11%)
  between operations  13.2 us (7%)
  starting transfers between devices  10.6 us (6%)
  other arithmetic  3.25 us (2%)
    conv_general_dilated x1, matrix products, on_device(): lax.conv_general_dilated(padded[None], kernel, (1, 1), 'VALID', dimension...  75.5 us
    ppermute x2, waiting for transfers between devices, extended(): lax.ppermute(lax.slice_in_dim(block, 0, width, axis=dim), axis, backward)  44.2 us
    all_gather x1, waiting for transfers between devices, on_device(): taps = lax.all_gather(dw_kernel, ('rows', 'cols'), axis=2, tiled=True)  14.1 us
    reshape x1, local copies, waits for them, and re-layouts, on_device(): kernel = taps.reshape(side, side, 1, channels)  12.8 us
    ppermute x2, starting transfers between devices, extended(): lax.ppermute(lax.slice_in_dim(block, block.shape[dim] - width, None, axis...  7.96 us
    dot_general x1, matrix products, reduce_back(): lax.dot_general(hidden, piece, (((1,), (1,)), ((), ())), preferred_elemen...  7.72 us
  transfers between devices with their start and end apart: 7, of which 3 were waited for; matrix products, arithmetic and copies ran while one was open for 51% of the time, Pallas kernels for 0%

commit v1 on v0

--- a/solution.py
+++ b/solution.py
@@ -31,7 +31,32 @@
 
 def on_device(features, dw_kernel, w_up, w_down):
     tile_rows, tile_cols, channels = features.shape
-    taps = lax.all_gather(dw_kernel, ("rows", "cols"), axis=2, tiled=True)
+    shaped, left_arr, formed = (
+        lax.axis_size(("rows", "cols")),
+        lax.axis_index(("rows", "cols")),
+        dw_kernel.shape[2],
+    )
+    leaves = [u * shaped if dev_i == 2 else u for dev_i, u in enumerate(dw_kernel.shape)]
+    taps = lax.dynamic_update_slice_in_dim(
+        jnp.zeros(leaves, dw_kernel.dtype), dw_kernel, left_arr * formed, axis=2
+    )
+    response = seen_now = dw_kernel
+    for num in tuple(range(1, shaped // 2 + 1)):
+        response = lax.ppermute(
+            response, ("rows", "cols"), [(dev_i, (dev_i + 1) % shaped) for dev_i in range(shaped)]
+        )
+        taps = lax.dynamic_update_slice_in_dim(
+            taps, response, (left_arr - num) % shaped * formed, axis=2
+        )
+        if 2 * num < shaped:
+            seen_now = lax.ppermute(
+                seen_now,
+                ("rows", "cols"),
+                [(dev_i, (dev_i - 1) % shaped) for dev_i in range(shaped)],
+            )
+            taps = lax.dynamic_update_slice_in_dim(
+                taps, seen_now, (left_arr + num) % shaped * formed, axis=2
+            )
     side = taps.shape[0]
     half = (side - 1) // 2
     padded = extended(features, (("rows", 0), ("cols", 1)), half)

time: 191 us -> 2620 us (13.72)
  local copies, waits for them, and re-layouts: 20.9 us -> 2370 us
  waiting for transfers between devices: 59 us -> 106 us
    dynamic_update_slice x0 -> x16, local copies, waits for them, and re-layouts: none -> 2340 us  [the longest x8 1170 us: on_device(): lax.dynamic_update_slice_in_dim(taps, response, (left_arr - num) % shaped...]
    ppermute x0 -> x15, waiting for transfers between devices: none -> 101 us  [the longest x8 63.3 us: on_device(): lax.ppermute(response, ('rows', 'cols'), [(dev_i, (dev_i + 1) % shaped) f...]
    ppermute x2, waiting for transfers between devices: 44.2 us -> 4.27 us  [extended(): lax.ppermute(lax.slice_in_dim(block, 0, width, axis=dim), axis, backward)]
  transfers between devices with their start and end apart: 7 -> 21, of which waited for: 3 -> 14; matrix products, arithmetic and copies ran while one was open for 51% -> 94% of each run, Pallas kernels for 0% -> 0%
where the time goes in v1:
time: 2620 us; the launch traced here: 2600 us
  local copies, waits for them, and re-layouts  2370 us (90%)
  waiting for transfers between devices  106 us (4%)
  matrix products  83.3 us (3%)
    dynamic_update_slice x8, local copies, waits for them, and re-layouts, on_device(): lax.dynamic_update_slice_in_dim(taps, response, (left_arr - num) % shaped...  1170 us
    dynamic_update_slice x7, local copies, waits for them, and re-layouts, on_device(): lax.dynamic_update_slice_in_dim(taps, seen_now, (left_arr + num) % shaped...  1140 us
    conv_general_dilated x1, matrix products, on_device(): lax.conv_general_dilated(padded[None], kernel, (1, 1), 'VALID', dimension...  75.6 us
    ppermute x8, waiting for transfers between devices, on_device(): lax.ppermute(response, ('rows', 'cols'), [(dev_i, (dev_i + 1) % shaped) f...  63.3 us
  transfers between devices with their start and end apart: 21, of which 14 were waited for; matrix products, arithmetic and copies ran while one was open for 94% of the time, Pallas kernels for 0%

profile of v1, /device:TPU:0, one launch (start us, length us, event | category | flops | bytes accessed | tf_op | source)
XLA Modules:
  0.0 2599.8 jit_solution(3536918129881979261)
XLA Ops:
  8.5 2.4 collective-permute-start
  12.3 4.3 collective-permute-done.1
  17.4 4.6 collective-permute-start.2
  22.1 1.4 copy.39
  24.8 2.7 collective-permute-start.4
  27.5 1.8 collective-permute-start.5
  29.3 37.7 %collective-permute-done.4 = bf16[31,31,48]{2,1,0:T(8,128)(2,1)} collective-permute-done((bf16[31,31,48]{2,1,0:T(8,128)(2,1)S(1)}, bf16[31,31,48]{2,1,0:T(8,128)(2,1)}, u32[]{:S(2)}, u32[]{:S(2)}) %collective-permute-start.4) | collective-permute-done | bytes 92288 | tf_op jit(solution)/shard_map/ppermute | solution.py:45
  66.9 2.3 collective-permute-done.5
  69.3 2.2 collective-permute-start.7
  71.5 6.8 collective-permute-done.6
  78.4 2.5 collective-permute-done.7
  80.8 2.1 collective-permute-start.9
  83.0 6.4 collective-permute-done.8
  89.4 5.0 collective-permute-done.9
  95.1 5.2 collective-permute-done.10
  100.3 7.2 collective-permute-done.11
  107.5 4.0 collective-permute-done.12
  111.5 9.8 collective-permute-done.13
  121.3 1.9 collective-permute-done.14
  123.3 10.5 collective-permute-done.15
  136.7 3.1 reshape.105
  139.8 34.9 %dynamic_update_slice.64 = bf16[31,31,1,768]{3,2,1,0:T(2,128)(2,1)} dynamic-update-slice(bf16[31,31,1,768]{3,2,1,0:T(2,128)(2,1)} %reshape.105, bf16[31,31,1,48]{3,2,1,0:T(2,128)(2,1)S(1)} %copy.42, s32[]{:T(128)} %constant.145.clone.1, s32[]{:T(128)} %constant.145.clone.1, s32[]{:T(128)} %constant.145.clone.1, s32[]{:T(128)S(6)} %select_n.111) | dynamic-update-slice | bytes 184516 | tf_op jit(solution)/shard_map/dynamic_update_slice | solution.py:40
  176.1 1.3 copy.44
  177.5 162.0 %dynamic_update_slice.65 = bf16[31,31,1,768]{3,2,1,0:T(2,128)(2,1)} dynamic-update-slice(bf16[31,31,1,768]{3,2,1,0:T(2,128)(2,1)} %dynamic_update_slice.64, bf16[31,31,1,48]{3,2,1,0:T(2,128)(2,1)S(1)} %copy.43, s32[]{:T(128)} %constant.145.clone.1, s32[]{:T(128)} %constant.145.clone.1, s32[]{:T(128)} %constant.145.clone.1, s32[]{:T(128)S(6)} %select_n.113) | dynamic-update-slice | bytes 184516 | tf_op jit(solution)/shard_map/dynamic_update_slice | solution.py:48
  339.4 162.5 %dynamic_update_slice.66 = bf16[31,31,1,768]{3,2,1,0:T(2,128)(2,1)} dynamic-update-slice(bf16[31,31,1,768]{3,2,1,0:T(2,128)(2,1)} %dynamic_update_slice.65, bf16[31,31,1,48]{3,2,1,0:T(2,128)(2,1)S(1)} %copy.44, s32[]{:T(128)} %constant.145.clone.1, s32[]{:T(128)} %constant.145.clone.1, s32[]{:T(128)} %constant.145.clone.1, s32[]{:T(128)S(6)} %select_n.115) | dynamic-update-slice | bytes 184516 | tf_op jit(solution)/shard_map/dynamic_update_slice | solution.py:57
  503.3 1.3 copy.46
  504.6 162.0 %dynamic_update_slice.67 = bf16[31,31,1,768]{3,2,1,0:T(2,128)(2,1)} dynamic-update-slice(bf16[31,31,1,768]{3,2,1,0:T(2,128)(2,1)} %dynamic_update_slice.66, bf16[31,31,1,48]{3,2,1,0:T(2,128)(2,1)S(1)} %copy.45, s32[]{:T(128)} %constant.145.clone.1, s32[]{:T(128)} %constant.145.clone.1, s32[]{:T(128)} %constant.145.clone.1, s32[]{:T(128)S(6)} %select_n.117) | dynamic-update-slice | bytes 184516 | tf_op jit(solution)/shard_map/dynamic_update_slice | solution.py:48
  666.6 162.5 %dynamic_update_slice.68 = bf16[31,31,1,768]{3,2,1,0:T(2,128)(2,1)} dynamic-update-slice(bf16[31,31,1,768]{3,2,1,0:T(2,128)(2,1)} %dynamic_update_slice.67, bf16[31,31,1,48]{3,2,1,0:T(2,128)(2,1)S(1)} %copy.46, s32[]{:T(128)} %constant.145.clone.1, s32[]{:T(128)} %constant.145.clone.1, s32[]{:T(128)} %constant.145.clone.1, s32[]{:T(128)S(6)} %select_n.119) | dynamic-update-slice | bytes 184516 | tf_op jit(solution)/shard_map/dynamic_update_slice | solution.py:57
  830.5 1.3 copy.48
  831.8 162.8 %dynamic_update_slice.69 = bf16[31,31,1,768]{3,2,1,0:T(2,128)(2,1)} dynamic-update-slice(bf16[31,31,1,768]{3,2,1,0:T(2,128)(2,1)} %dynamic_update_slice.68, bf16[31,31,1,48]{3,2,1,0:T(2,128)(2,1)S(1)} %copy.47, s32[]{:T(128)} %constant.145.clone.1, s32[]{:T(128)} %constant.145.clone.1, s32[]{:T(128)} %constant.145.clone.1, s32[]{:T(128)S(6)} %select_n.121) | dynamic-update-slice | bytes 184516 | tf_op jit(solution)/shard_map/dynamic_update_slice | solution.py:48
  994.6 162.5 %dynamic_update_slice.70 = bf16[31,31,1,768]{3,2,1,0:T(2,128)(2,1)} dynamic-update-slice(bf16[31,31,1,768]{3,2,1,0:T(2,128)(2,1)} %dynamic_update_slice.69, bf16[31,31,1,48]{3,2,1,0:T(2,128)(2,1)S(1)} %copy.48, s32[]{:T(128)} %constant.145.clone.1, s32[]{:T(128)} %constant.145.clone.1, s32[]{:T(128)} %constant.145.clone.1, s32[]{:T(128)S(6)} %select_n.123) | dynamic-update-slice | bytes 184516 | tf_op jit(solution)/shard_map/dynamic_update_slice | solution.py:57
  1158.4 1.3 copy.50
  1159.7 162.5 %dynamic_update_slice.71 = bf16[31,31,1,768]{3,2,1,0:T(2,128)(2,1)} dynamic-update-slice(bf16[31,31,1,768]{3,2,1,0:T(2,128)(2,1)} %dynamic_update_slice.70, bf16[31,31,1,48]{3,2,1,0:T(2,128)(2,1)S(1)} %copy.49, s32[]{:T(128)} %constant.145.clone.1, s32[]{:T(128)} %constant.145.clone.1, s32[]{:T(128)} %constant.145.clone.1, s32[]{:T(128)S(6)} %select_n.125) | dynamic-update-slice | bytes 184516 | tf_op jit(solution)/shard_map/dynamic_update_slice | solution.py:48
  1322.3 162.5 %dynamic_update_slice.72 = bf16[31,31,1,768]{3,2,1,0:T(2,128)(2,1)} dynamic-update-slice(bf16[31,31,1,768]{3,2,1,0:T(2,128)(2,1)} %dynamic_update_slice.71, bf16[31,31,1,48]{3,2,1,0:T(2,128)(2,1)S(1)} %copy.50, s32[]{:T(128)} %constant.145.clone.1, s32[]{:T(128)} %constant.145.clone.1, s32[]{:T(128)} %constant.145.clone.1, s32[]{:T(128)S(6)} %select_n.127) | dynamic-update-slice | bytes 184516 | tf_op jit(solution)/shard_map/dynamic_update_slice | solution.py:57
  1486.1 1.3 copy.52
  1487.5 162.5 %dynamic_update_slice.73 = bf16[31,31,1,768]{3,2,1,0:T(2,128)(2,1)} dynamic-update-slice(bf16[31,31,1,768]{3,2,1,0:T(2,128)(2,1)} %dynamic_update_slice.72, bf16[31,31,1,48]{3,2,1,0:T(2,128)(2,1)S(1)} %copy.51, s32[]{:T(128)} %constant.145.clone.1, s32[]{:T(128)} %constant.145.clone.1, s32[]{:T(128)} %constant.145.clone.1, s32[]{:T(128)S(6)} %select_n.129) | dynamic-update-slice | bytes 184516 | tf_op jit(solution)/shard_map/dynamic_update_slice | solution.py:48
  1650.0 162.9 %dynamic_update_slice.74 = bf16[31,31,1,768]{3,2,1,0:T(2,128)(2,1)} dynamic-update-slice(bf16[31,31,1,768]{3,2,1,0:T(2,128)(2,1)} %dynamic_update_slice.73, bf16[31,31,1,48]{3,2,1,0:T(2,128)(2,1)S(1)} %copy.52, s32[]{:T(128)} %constant.145.clone.1, s32[]{:T(128)} %constant.145.clone.1, s32[]{:T(128)} %constant.145.clone.1, s32[]{:T(128)S(6)} %select_n.131) | dynamic-update-slice | bytes 184516 | tf_op jit(solution)/shard_map/dynamic_update_slice | solution.py:57
  1815.6 162.6 %dynamic_update_slice.75 = bf16[31,31,1,768]{3,2,1,0:T(2,128)(2,1)} dynamic-update-slice(bf16[31,31,1,768]{3,2,1,0:T(2,128)(2,1)} %dynamic_update_slice.74, bf16[31,31,1,48]{3,2,1,0:T(2,128)(2,1)S(1)} %copy.53, s32[]{:T(128)} %constant.145.clone.1, s32[]{:T(128)} %constant.145.clone.1, s32[]{:T(128)} %constant.145.clone.1, s32[]{:T(128)S(6)} %select_n.133) | dynamic-update-slice | bytes 184516 | tf_op jit(solution)/shard_map/dynamic_update_slice | solution.py:48
  1978.1 162.5 %dynamic_update_slice.76 = bf16[31,31,1,768]{3,2,1,0:T(2,128)(2,1)} dynamic-update-slice(bf16[31,31,1,768]{3,2,1,0:T(2,128)(2,1)} %dynamic_update_slice.75, bf16[31,31,1,48]{3,2,1,0:T(2,128)(2,1)S(1)} %copy.54, s32[]{:T(128)} %constant.145.clone.1, s32[]{:T(128)} %constant.145.clone.1, s32[]{:T(128)} %constant.145.clone.1, s32[]{:T(128)S(6)} %select_n.135) | dynamic-update-slice | bytes 184516 | tf_op jit(solution)/shard_map/dynamic_update_slice | solution.py:57
  2141.0 1.3 copy.56
  2142.4 162.6 %dynamic_update_slice.77 = bf16[31,31,1,768]{3,2,1,0:T(2,128)(2,1)} dynamic-update-slice(bf16[31,31,1,768]{3,2,1,0:T(2,128)(2,1)} %dynamic_update_slice.76, bf16[31,31,1,48]{3,2,1,0:T(2,128)(2,1)S(1)} %copy.55, s32[]{:T(128)} %constant.145.clone.1, s32[]{:T(128)} %constant.145.clone.1, s32[]{:T(128)} %constant.145.clone.1, s32[]{:T(128)S(6)} %select_n.137) | dynamic-update-slice | bytes 184516 | tf_op jit(solution)/shard_map/dynamic_update_slice | solution.py:48
  2304.9 162.5 %dynamic_update_slice.78 = bf16[31,31,1,768]{3,2,1,0:T(2,128)(2,1)} dynamic-update-slice(bf16[31,31,1,768]{3,2,1,0:T(2,128)(2,1)} %dynamic_update_slice.77, bf16[31,31,1,48]{3,2,1,0:T(2,128)(2,1)S(1)} %copy.56, s32[]{:T(128)} %constant.145.clone.1, s32[]{:T(128)} %constant.145.clone.1, s32[]{:T(128)} %constant.145.clone.1, s32[]{:T(128)S(6)} %select_n.139) | dynamic-update-slice | bytes 184516 | tf_op jit(solution)/shard_map/dynamic_update_slice | solution.py:57
  2468.8 34.8 %dynamic_update_slice.79 = bf16[31,31,1,768]{3,2,1,0:T(2,128)(2,1)} dynamic-update-slice(bf16[31,31,1,768]{3,2,1,0:T(2,128)(2,1)} %dynamic_update_slice.78, bf16[31,31,1,48]{3,2,1,0:T(2,128)(2,1)S(1)} %copy.57, s32[]{:T(128)} %constant.145.clone.1, s32[]{:T(128)} %constant.145.clone.1, s32[]{:T(128)} %constant.145.clone.1, s32[]{:T(128)S(6)} %select_n.141) | dynamic-update-slice | bytes 184516 | tf_op jit(solution)/shard_map/dynamic_update_slice | solution.py:48
  2503.6 1.6 copy.40
  2505.2 1.6 copy.41
  2506.8 1.4 maximum_bitcast_fusion
  2508.6 75.6 %fusion = f32[1,16,16,768]{3,0,2,1:T(1,128)S(1)} fusion(bf16[31,31,1,768]{3,2,1,0:T(2,128)(2,1)S(1)} %copy-done.2, bf16[1,46,46,768]{3,2,1,0:T(8,128)(2,1)S(1)} %maximum_bitcast_fusion), kind=kOutput, calls=%fused_computation | convolution fusion | flops 377880576 | bytes 5512704 | tf_op jit(solution)/shard_map/conv_general_dilated | solution.py:64
  2585.0 7.7 fusion.12
  (72 shorter events, 21.0 us)
Async XLA Ops:
  6.5 5.7 copy-start
  6.5 2578.5 %all-gather.3.cloned.1.call-start = ((), (), s32[]{:S(2)}) async-start(), calls=%async_computation | async-start | bytes 2506752 | tf_op jit(solution)/shard_map/all_gather | solution.py:78
  7.3 2577.8 %all-gather.5.cloned.1.call-start = ((), (), s32[]{:S(2)}) async-start(), calls=%async_computation.1 | async-start | bytes 2506752 | tf_op jit(solution)/shard_map/all_gather | solution.py:79
  8.5 3.7 collective-permute-start
  10.9 5.7 collective-permute-start.1
  17.4 7.3 copy-start.3
  17.4 2486.2 %collective-permute-start.2 = (bf16[46,15,768]{2,0,1:T(8,128)(2,1)S(1)}, bf16[46,15,768]{2,0,1:T(8,128)(2,1)}, u32[]{:S(2)}, u32[]{:S(2)}) collective-permute-start(bf16[46,15,768]{2,0,1:T(8,128)(2,1)S(1)} %copy.38), channel_id=1, source_target_pairs={{0,1},{1,2},{2,3},{4,5},{5,6},{6,7},{8,9},{9,10},{10,11},{12,13},{... | collective-permute-start | bytes 3179528 | tf_op jit(solution)/shard_map/ppermute | solution.py:12
  23.5 2481.7 %collective-permute-start.3 = (bf16[46,15,768]{2,0,1:T(8,128)(2,1)}, bf16[46,15,768]{2,0,1:T(8,128)(2,1)}, u32[]{:S(2)}, u32[]{:S(2)}) collective-permute-start(bf16[46,15,768]{2,0,1:T(8,128)(2,1)} %copy.39), channel_id=1, source_target_pairs={{1,0},{2,1},{3,2},{5,4},{6,5},{7,6},{9,8},{10,9},{11,10},{13,12},{... | collective-permute-start | bytes 3179528 | tf_op jit(solution)/shard_map/ppermute | solution.py:15
  24.8 42.2 %collective-permute-start.4 = (bf16[31,31,48]{2,1,0:T(8,128)(2,1)S(1)}, bf16[31,31,48]{2,1,0:T(8,128)(2,1)}, u32[]{:S(2)}, u32[]{:S(2)}) collective-permute-start(bf16[31,31,48]{2,1,0:T(8,128)(2,1)S(1)} %copy-done.3), channel_id=1, source_target_pairs={{0,1},{1,2},{2,3},{3,4},{4,5},{5,6},{6,7},{7,8},{8,9},{9,10},{10,1... | collective-permute-start | bytes 276776 | tf_op jit(solution)/shard_map/ppermute | solution.py:45
  27.5 41.8 %collective-permute-start.5 = (bf16[31,31,48]{2,1,0:T(8,128)(2,1)S(1)}, bf16[31,31,48]{2,1,0:T(8,128)(2,1)S(1)}, u32[]{:S(2)}, u32[]{:S(2)}) collective-permute-start(bf16[31,31,48]{2,1,0:T(8,128)(2,1)S(1)} %copy-done.3), channel_id=1, source_target_pairs={{0,15},{1,0},{2,1},{3,2},{4,3},{5,4},{6,5},{7,6},{8,7},{9,8},{10,9... | collective-permute-start | bytes 276776 | tf_op jit(solution)/shard_map/ppermute | solution.py:52
  66.9 11.4 collective-permute-start.6
  69.3 65.8 %copy-start.4 = (bf16[31,31,48]{2,1,0:T(8,128)(2,1)}, bf16[31,31,48]{2,1,0:T(8,128)(2,1)S(1)}, u32[]{:S(2)}) copy-start(bf16[31,31,48]{2,1,0:T(8,128)(2,1)S(1)} %collective-permute-done.5) | copy-start | bytes 276772
  69.3 11.6 collective-permute-start.7
  78.4 11.0 collective-permute-start.8
  80.8 54.3 %copy-start.6 = (bf16[31,31,48]{2,1,0:T(8,128)(2,1)}, bf16[31,31,48]{2,1,0:T(8,128)(2,1)S(1)}, u32[]{:S(2)}) copy-start(bf16[31,31,48]{2,1,0:T(8,128)(2,1)S(1)} %collective-permute-done.7) | copy-start | bytes 276772
  80.8 13.5 collective-permute-start.9
  89.4 10.9 collective-permute-start.10
  94.4 40.7 %copy-start.8 = (bf16[31,31,48]{2,1,0:T(8,128)(2,1)}, bf16[31,31,48]{2,1,0:T(8,128)(2,1)S(1)}, u32[]{:S(2)}) copy-start(bf16[31,31,48]{2,1,0:T(8,128)(2,1)S(1)} %collective-permute-done.9) | copy-start | bytes 276772
  94.4 13.1 collective-permute-start.11
  100.3 34.8 %copy-start.5 = (bf16[31,31,48]{2,1,0:T(8,128)(2,1)}, bf16[31,31,48]{2,1,0:T(8,128)(2,1)S(1)}, u32[]{:S(2)}) copy-start(bf16[31,31,48]{2,1,0:T(8,128)(2,1)S(1)} %collective-permute-done.10) | copy-start | bytes 276772
  100.3 11.2 collective-permute-start.12
  107.5 27.6 %copy-start.10 = (bf16[31,31,48]{2,1,0:T(8,128)(2,1)}, bf16[31,31,48]{2,1,0:T(8,128)(2,1)S(1)}, u32[]{:S(2)}) copy-start(bf16[31,31,48]{2,1,0:T(8,128)(2,1)S(1)} %collective-permute-done.11) | copy-start | bytes 276772
  107.5 13.8 collective-permute-start.13
  111.5 23.7 copy-start.7
  111.5 11.8 collective-permute-start.14
  121.3 13.8 copy-start.11
  121.3 12.5 collective-permute-start.15
  123.2 11.9 copy-start.9
  123.2 11.9 collective-permute-start.16
  133.8 2007.2 %collective-permute-start.17 = (bf16[31,31,48]{2,1,0:T(8,128)(2,1)}, bf16[31,31,48]{2,1,0:T(8,128)(2,1)}, u32[]{:S(2)}, u32[]{:S(2)}) collective-permute-start(bf16[31,31,48]{2,1,0:T(8,128)(2,1)} %collective-permute-done.15), channel_id=1, source_target_pairs={{0,15},{1,0},{2,1},{3,2},{4,3},{5,4},{6,5},{7,6},{8,7},{9,8},{10,9... | collective-permute-start | bytes 276776 | tf_op jit(solution)/shard_map/ppermute | solution.py:52
  135.2 2332.3 %collective-permute-start.18 = (bf16[31,31,48]{2,1,0:T(8,128)(2,1)S(1)}, bf16[31,31,48]{2,1,0:T(8,128)(2,1)}, u32[]{:S(2)}, u32[]{:S(2)}) collective-permute-start(bf16[31,31,48]{2,1,0:T(8,128)(2,1)S(1)} %collective-permute-done.16), channel_id=1, source_target_pairs={{0,1},{1,2},{2,3},{3,4},{4,5},{5,6},{6,7},{7,8},{8,9},{9,10},{10,1... | collective-permute-start | bytes 276776 | tf_op jit(solution)/shard_map/ppermute | solution.py:45
  2506.8 1.8 copy-start.2
  2508.6 75.6 %copy-start.1 = (bf16[16,16,768]{2,1,0:T(8,128)(2,1)S(1)}, bf16[16,16,768]{2,1,0:T(8,128)(2,1)}, u32[]{:S(2)}) copy-start(bf16[16,16,768]{2,1,0:T(8,128)(2,1)} %param.4) | copy-start | bytes 1179652
Sparse Core Ops, SparseCore 0:
  9.6 50.2 all-gather.2
  136.1 60.7 all-gather.4
